TPU v7x, 512 devices: a whole 4x4x16 slice. The times are simulated.
512 devices in a mesh: dp: 4 (over y), outer: 32 (over z, core), inner: 4 (over x).
Axes of the slice: x: 4, y: 4, z: 16, core: 2. Of those that a mesh axis runs over, the one named last changes fastest.
Arguments:
- query_rows: bfloat16 [65536, 256], P(('dp', 'outer', 'inner')), parts along dimension 0, may hold values from -8 to 8
- key_rows: bfloat16 [65536, 256], P(('dp', 'outer', 'inner')), parts along dimension 0, may hold values from -8 to 8
- value_rows: bfloat16 [65536, 1024], P(('dp', 'outer', 'inner')), parts along dimension 0, may hold values from -6 to 6
- conv_weight: float32 [3, 1024], replicated, may hold values from -1 to 1
- norm_gain: float32 [1024], replicated, may hold values from 0.1 to 1.9
Outputs:
- layer_out: bfloat16 [65536, 1024], P(('dp', 'outer', 'inner')), parts along dimension 0
There are 4 independent parts, one for each index of `dp`. A program takes and returns all parts, laid end to end along the dimension named above; an argument that names none is the same for every part. Nothing has to cross between parts.
All inputs are finite; a program needn't handle non-finite values.
Results may differ from a plain program's by a relative error of at most 0.013.
Values may be sent and summed in bfloat16 or wider, within the bound.
No kernel may reach another device: no remote copies, remote signals or barrier semaphores. Data moves between devices by JAX's collectives and lax.ppermute only.
A program may use at most 128 MiB of HBM per device.

v0:
```python
import math
import jax
import jax.numpy as jnp
from jax import lax
from jax.sharding import PartitionSpec as P

HEADS = 16
FEAT = 16
VDIM = 64
PHI = 273
TAPS = 3
WIN = 64
BLK = 128


def shifted(value, axis, steps):
    count = lax.axis_size(axis)
    initial, last = (max(0, -steps), min(count, count - steps))
    return lax.ppermute(value, axis, [(source, source + steps) for source in range(initial, last)])


def carried_in(shard, axis, combine, identity):
    count, position = (lax.axis_size(axis), lax.axis_index(axis))
    everything = lax.all_gather(shard.astype(jnp.bfloat16), axis)
    start = jnp.broadcast_to(jnp.asarray(identity, shard.dtype), shard.shape)

    def hop(k, before):
        reached = k < position
        new = combine(before, everything[k].astype(shard.dtype))
        return jnp.where(reached, new, before)

    return lax.fori_loop(0, count, hop, start)


def features(rows_in):
    entries = rows_in.astype(jnp.float32)
    leading = entries.shape[:-1]
    pair_terms = (entries[..., :, None] * entries[..., None, :]).reshape(leading + (FEAT * FEAT,))
    const_term = jnp.ones(leading + (1,), jnp.float32)
    joined = jnp.concatenate(
        [const_term, entries * (1.0 / FEAT**0.25), pair_terms * (1.0 / math.sqrt(2.0 * FEAT))],
        axis=-1,
    )
    return joined.astype(jnp.bfloat16)


def convolve(padded, conv_weight, out_rows):
    conv_sum = jnp.zeros((out_rows, padded.shape[1]), jnp.float32)
    for tap_index in range(TAPS):
        offset = TAPS - 1 - tap_index
        conv_sum = conv_sum + conv_weight[tap_index][None, :] * padded[
            offset : offset + out_rows
        ].astype(jnp.float32)
    return conv_sum.astype(jnp.bfloat16)


def add_states(earlier_part, later_part):
    return earlier_part + later_part


def on_device(query_rows, key_rows, value_rows, conv_weight, norm_gain):
    local_rows = query_rows.shape[0]
    lag_rows = TAPS - 1
    score_scale = 1.0 / math.sqrt(FEAT)
    block_index = lax.axis_index(("outer", "inner"))
    tail_conv = convolve(value_rows[local_rows - WIN - lag_rows :], conv_weight, WIN)
    prev_keys, prev_conv, prev_raw = shifted(
        (key_rows[local_rows - WIN :], tail_conv, value_rows[local_rows - lag_rows :]),
        ("outer", "inner"),
        1,
    )
    conv_rows = convolve(jnp.concatenate([prev_raw, value_rows], 0), conv_weight, local_rows)
    block_total = local_rows // BLK
    query_blocks = query_rows.reshape(block_total, BLK, HEADS, FEAT)
    key_blocks = key_rows.reshape(block_total, BLK, HEADS, FEAT)
    value_blocks = conv_rows.reshape(block_total, BLK, HEADS, VDIM)
    phi_key = features(key_blocks)
    block_states = jnp.einsum(
        "ntaf,ntac->nfac", phi_key, value_blocks, preferred_element_type=jnp.float32
    )
    local_before = jnp.concatenate(
        [jnp.zeros_like(block_states), jnp.cumsum(block_states[:-1], axis=0)], 0
    )
    local_total = local_before[-1] + block_states[-1]
    scores = (
        jnp.einsum("niaf,njaf->naij", query_blocks, key_blocks, preferred_element_type=jnp.float32)
        * score_scale
    )
    causal = jnp.arange(BLK)[:, None] >= jnp.arange(BLK)[None, :]
    intra_weights = jnp.where(causal[None, None], 1.0 + scores + 0.5 * scores * scores, 0.0).astype(
        jnp.bfloat16
    )
    own_part = jnp.einsum(
        "naij,njac->niac", intra_weights, value_blocks, preferred_element_type=jnp.float32
    )
    win_blocks = local_rows // WIN
    ext_keys = jnp.concatenate([prev_keys, key_rows], 0).reshape(win_blocks + 1, WIN, HEADS, FEAT)
    ext_conv = jnp.concatenate([prev_conv, conv_rows], 0).reshape(win_blocks + 1, WIN, HEADS, VDIM)
    near_keys = jnp.concatenate([ext_keys[:-1], ext_keys[1:]], axis=1)
    near_values = jnp.concatenate([ext_conv[:-1], ext_conv[1:]], axis=1)
    query_windows = query_rows.reshape(win_blocks, WIN, HEADS, FEAT)
    window_scores = (
        jnp.einsum("niaf,njaf->naij", query_windows, near_keys, preferred_element_type=jnp.float32)
        * score_scale
    )
    offset_rows = jnp.arange(2 * WIN)[None, :] - jnp.arange(WIN)[:, None]
    inside = (offset_rows >= 0) & (offset_rows <= WIN)
    position = (
        block_index * local_rows
        + jnp.arange(win_blocks, dtype=jnp.int32)[:, None] * WIN
        + jnp.arange(2 * WIN, dtype=jnp.int32)[None, :]
        - WIN
    )
    allowed = inside[None, None] & (position >= 0)[:, None, None, :]
    masked = jnp.where(allowed, window_scores, -1e30)
    row_max = jnp.max(masked, axis=-1, keepdims=True)
    exp_scores = jnp.where(allowed, jnp.exp(masked - row_max), 0.0)
    window_probs = (exp_scores / jnp.sum(exp_scores, axis=-1, keepdims=True)).astype(jnp.bfloat16)
    window_out = jnp.einsum(
        "naij,njac->niac", window_probs, near_values, preferred_element_type=jnp.float32
    )
    sent_state = local_total.reshape(PHI, HEADS * VDIM)
    zero_state = jnp.zeros(sent_state.shape, jnp.float32)
    group_sum = None
    inner_prefix = carried_in(sent_state, "inner", add_states, zero_state)
    group_sum = lax.psum(sent_state, "inner")
    outer_before = carried_in(group_sum, "outer", add_states, zero_state)
    carried = inner_prefix + outer_before
    carried = carried.reshape(PHI, HEADS, VDIM)
    state_rounded = (carried[None] + local_before).astype(jnp.bfloat16)
    phi_query = features(query_blocks)
    earlier_part = jnp.einsum(
        "ntaf,nfac->ntac", phi_query, state_rounded, preferred_element_type=jnp.float32
    )
    numerator = (own_part + earlier_part).reshape(local_rows, HEADS, VDIM)
    mean_square = jnp.mean(numerator * numerator, axis=-1, keepdims=True)
    linear_out = numerator * lax.rsqrt(mean_square + 1e-06) * norm_gain.reshape(HEADS, VDIM)
    mixed_heads = linear_out + window_out.reshape(local_rows, HEADS, VDIM)
    return mixed_heads.astype(jnp.bfloat16).reshape(local_rows, HEADS * VDIM)


def solution(mesh):
    in_specs = (
        P(("dp", "outer", "inner"), None),
        P(("dp", "outer", "inner"), None),
        P(("dp", "outer", "inner"), None),
        P(),
        P(),
    )
    out_specs = P(("dp", "outer", "inner"), None)
    return jax.shard_map(
        on_device, mesh=mesh, in_specs=in_specs, out_specs=out_specs, check_vma=False
    )
```

profile of v0, /device:TPU:1, one launch (start us, length us, event | category | flops | bytes accessed | tf_op | source)
XLA Modules:
  0.0 259.6 jit_solution(5805641317175301192)
XLA Ops:
  7.5 3.9 %collective-permute-start = (bf16[2,1024]{0,1:T(8,128)(2,1)S(1)}, bf16[2,1024]{0,1:T(8,128)(2,1)S(1)}, u32[]{:S(2)}, u32[]{:S(2)}) collective-permute-start(bf16[2,1024]{0,1:T(8,128)(2,1)S(1)} %copy.66), channel_id=1, source_target_pairs={{0,1},{1,2},{2,3},{3,4},{4,5},{5,6},{6,7},{7,8},{8,9},{9,10},{10,1... | collective-permute-start | bytes 12296 | tf_op jit(solution)/shard_map/ppermute | solution.py:19
  13.0 4.3 %collective-permute-done = bf16[2,1024]{0,1:T(8,128)(2,1)S(1)} collective-permute-done((bf16[2,1024]{0,1:T(8,128)(2,1)S(1)}, bf16[2,1024]{0,1:T(8,128)(2,1)S(1)}, u32[]{:S(2)}, u32[]{:S(2)}) %collective-permute-start) | collective-permute-done | bytes 4128 | tf_op jit(solution)/shard_map/ppermute | solution.py:19
  19.6 2.2 copy.70
  22.3 29.1 %all-reduce.1 = bf16[273,1024]{1,0:T(8,128)(2,1)} all-reduce(f32[273,1024]{1,0:T(8,128)S(1)} %copy.71), channel_id=1, replica_groups=mesh['dp'=4,'outer'=32,'inner'=4] {'inner'}, use_global_device_ids=true, to_apply=%region_2.3 | all-reduce | flops 279552 | bytes 1677312 | tf_op jit(solution)/shard_map/psum | solution.py:126
  52.8 2.1 collective-permute-start.1
  55.0 2.3 collective-permute-start.2
  63.2 10.6 %collective-permute-done.2 = bf16[64,256]{1,0:T(8,128)(2,1)S(1)} collective-permute-done((bf16[64,256]{1,0:T(8,128)(2,1)S(1)}, bf16[64,256]{1,0:T(8,128)(2,1)S(1)}, u32[]{:S(2)}, u32[]{:S(2)}) %collective-permute-start.2) | collective-permute-done | bytes 32800 | tf_op jit(solution)/shard_map/ppermute | solution.py:19
  74.1 1.9 fusion.77
  77.5 6.4 %convolution_bitcast_fusion = f32[2,64,16,64]{1,3,2,0:T(8,128)} fusion(bf16[2,64,16,64]{1,3,2,0:T(8,128)(2,1)} %copy.79, bf16[2,64,16,64]{1,3,2,0:T(8,128)(2,1)S(1)} %copy.78, f32[2,16,64]{2,1,0:T(8,128)S(1)} %fusion.77, pred[2,64,128]{2,1,0:T(8,128)(4,1)S(1)} %broadcast_and_fusion, bf16[2,64,16,16]{1,3,2,0:T(8,128)(2,1)} %copy.83, ...), kind=kOutput, calls=%fused_computation.9 | convolution fusion | flops 44828800 | bytes 1269760 | tf_op jit(solution)/shard_map/naij,njac->niac/dot_general | solution.py:119
  83.9 2.0 copy.93
  87.3 6.8 %while.28 = (s32[]{:T(128)}, f32[273,1024]{1,0:T(8,128)S(1)}, s32[]{:T(128)}, bf16[4,273,1024]{2,1,0:T(8,128)(2,1)}, s32[]{:T(128)}, /*index=5*/s32[]{:T(128)}) while((s32[]{:T(128)}, f32[273,1024]{1,0:T(8,128)S(1)}, s32[]{:T(128)}, bf16[4,273,1024]{2,1,0:T(8,128)(2,1)}, s32[]{:T(128)}, /*index=5*/s32[]{:T(128)}) %tuple.63), condition=%wide.region_1.2_spmd.clone, body=%wide.region_0.1_spmd.clone.sunk | while | flops 1118212 | bytes 2795613 | solution.py:32
  87.3 1.7 add_select_fusion.4
  89.0 1.7 add_select_fusion.4
  90.7 1.7 add_select_fusion.4
  92.4 1.7 add_select_fusion.4
  94.1 100.6 %all-gather.7.cloned.1.call-done = bf16[32,273,1024]{2,1,0:T(8,128)(2,1)} async-done(((bf16[1,273,1024]{2,1,0:T(8,128)(2,1)}), bf16[32,273,1024]{2,1,0:T(8,128)(2,1)}) %all-gather.7.cloned.1.call-update) | async-done | bytes 17891344 | tf_op jit(solution)/shard_map/all_gather | solution.py:24
  194.8 54.4 %while.29 = (s32[]{:T(128)}, f32[273,1024]{1,0:T(8,128)S(1)}, s32[]{:T(128)}, bf16[32,273,1024]{2,1,0:T(8,128)(2,1)}, s32[]{:T(128)}, /*index=5*/s32[]{:T(128)}) while((s32[]{:T(128)}, f32[273,1024]{1,0:T(8,128)S(1)}, s32[]{:T(128)}, bf16[32,273,1024]{2,1,0:T(8,128)(2,1)}, s32[]{:T(128)}, /*index=5*/s32[]{:T(128)}) %tuple.66), condition=%wide.region_4.5_spmd.clone, body=%wide.region_3.4_spmd.clone.sunk | while | flops 1118212 | bytes 2795613 | solution.py:32
  196.5 1.7 add_select_fusion.5
  198.2 1.7 add_select_fusion.5
  199.9 1.7 add_select_fusion.5
  201.6 1.7 add_select_fusion.5
  203.3 1.7 add_select_fusion.5
  205.0 1.7 add_select_fusion.5
  206.7 1.7 add_select_fusion.5
  208.4 1.7 add_select_fusion.5
  210.1 1.7 add_select_fusion.5
  211.8 1.7 add_select_fusion.5
  213.5 1.7 add_select_fusion.5
  215.2 1.7 add_select_fusion.5
  216.9 1.7 add_select_fusion.5
  218.6 1.7 add_select_fusion.5
  220.3 1.7 add_select_fusion.5
  222.0 1.7 add_select_fusion.5
  223.7 1.7 add_select_fusion.5
  225.4 1.7 add_select_fusion.5
  227.1 1.7 add_select_fusion.5
  228.8 1.7 add_select_fusion.5
  230.5 1.7 add_select_fusion.5
  232.2 1.7 add_select_fusion.5
  233.9 1.7 add_select_fusion.5
  235.6 1.7 add_select_fusion.5
  237.3 1.7 add_select_fusion.5
  239.0 1.7 add_select_fusion.5
  240.7 1.7 add_select_fusion.5
  242.4 1.7 add_select_fusion.5
  244.1 1.7 add_select_fusion.5
  245.8 1.7 add_select_fusion.5
  247.5 1.7 add_select_fusion.5
  (74 shorter events, 20.7 us)
Async XLA Ops:
  6.5 6.3 %copy-start.3 = (bf16[128,1024]{1,0:T(8,128)(2,1)S(1)}, bf16[128,1024]{1,0:T(8,128)(2,1)}, u32[]{:S(2)}) copy-start(bf16[128,1024]{1,0:T(8,128)(2,1)} %param.11) | copy-start | bytes 786436
  6.5 6.3 %copy-start.8 = (f32[3,1024]{1,0:T(4,128)S(1)}, f32[3,1024]{1,0:T(4,128)}, u32[]{:S(2)}) copy-start(f32[3,1024]{1,0:T(4,128)} %param.12) | copy-start | bytes 36868
  6.5 80.8 %all-gather.5.cloned.1.call-start = ((), (), s32[]{:S(2)}) async-start(), calls=%async_computation | async-start | bytes 2867200 | tf_op jit(solution)/shard_map/all_gather | solution.py:24
  7.5 9.8 %collective-permute-start = (bf16[2,1024]{0,1:T(8,128)(2,1)S(1)}, bf16[2,1024]{0,1:T(8,128)(2,1)S(1)}, u32[]{:S(2)}, u32[]{:S(2)}) collective-permute-start(bf16[2,1024]{0,1:T(8,128)(2,1)S(1)} %copy.66), channel_id=1, source_target_pairs={{0,1},{1,2},{2,3},{3,4},{4,5},{5,6},{6,7},{7,8},{8,9},{9,10},{10,1... | collective-permute-start | bytes 12296 | tf_op jit(solution)/shard_map/ppermute | solution.py:19
  21.9 172.9 %all-gather.7.cloned.1.call-start = ((), (), s32[]{:S(2)}) async-start(), calls=%async_computation.1 | async-start | bytes 18923520 | tf_op jit(solution)/shard_map/all_gather | solution.py:24
  51.4 3.6 %copy-start.2 = (bf16[128,256]{1,0:T(8,128)(2,1)S(1)}, bf16[128,256]{1,0:T(8,128)(2,1)}, u32[]{:S(2)}) copy-start(bf16[128,256]{1,0:T(8,128)(2,1)} %param.10) | copy-start | bytes 196612
  51.4 6.0 %copy-start.6 = (bf16[128,256]{1,0:T(8,128)(2,1)S(1)}, bf16[128,256]{1,0:T(8,128)(2,1)}, u32[]{:S(2)}) copy-start(bf16[128,256]{1,0:T(8,128)(2,1)} %param.9) | copy-start | bytes 196612
  52.8 23.2 %collective-permute-start.1 = (bf16[64,1024]{0,1:T(8,128)(2,1)}, bf16[64,1024]{0,1:T(8,128)(2,1)}, u32[]{:S(2)}, u32[]{:S(2)}) collective-permute-start(bf16[64,1024]{0,1:T(8,128)(2,1)} %add_convert_fusion.1), channel_id=1, source_target_pairs={{0,1},{1,2},{2,3},{3,4},{4,5},{5,6},{6,7},{7,8},{8,9},{9,10},{10,1... | collective-permute-start | bytes 393224 | tf_op jit(solution)/shard_map/ppermute | solution.py:19
  55.0 18.8 %collective-permute-start.2 = (bf16[64,256]{1,0:T(8,128)(2,1)S(1)}, bf16[64,256]{1,0:T(8,128)(2,1)S(1)}, u32[]{:S(2)}, u32[]{:S(2)}) collective-permute-start(bf16[64,256]{1,0:T(8,128)(2,1)S(1)} %slice.69), channel_id=1, source_target_pairs={{0,1},{1,2},{2,3},{3,4},{4,5},{5,6},{6,7},{7,8},{8,9},{9,10},{10,1... | collective-permute-start | bytes 98312 | tf_op jit(solution)/shard_map/ppermute | solution.py:19
  57.7 16.4 %copy-start.4 = (bf16[2,64,16,16]{1,0,3,2:T(2,128)(2,1)}, bf16[2,64,16,16]{1,0,3,2:T(2,128)(2,1)S(1)}, u32[]{:S(2)}) copy-start(bf16[2,64,16,16]{1,0,3,2:T(2,128)(2,1)S(1)} %reshape.244) | copy-start | bytes 196612
  74.1 1.9 copy-start.5
  249.2 1.0 copy-start.10
  249.4 1.3 copy-start.1
  249.4 1.3 copy-start.7
  250.7 1.0 copy-start
  250.7 1.0 copy-start.9
Sparse Core Ops, SparseCore 0:
  22.0 51.1 all-gather.4
  75.2 119.4 all-gather.6
where the time goes:
time: 262 us; the launch traced here: 260 us
  waiting for transfers between devices  116 us (44%)
  other arithmetic  66.4 us (25%)
  blocking collectives  29.1 us (11%)
  between operations  13.8 us (5%)
  local copies, waits for them, and re-layouts  13.5 us (5%)
  matrix products  12 us (5%)
  starting transfers between devices  8.44 us (3%)
    all_gather x2, waiting for transfers between devices, carried_in(): everything = lax.all_gather(shard.astype(jnp.bfloat16), axis)  101 us
    select_n x36, other arithmetic, hop(): return jnp.where(reached, new, before)  60.4 us
    psum x1, blocking collectives, on_device(): group_sum = lax.psum(sent_state, 'inner')  29.1 us
    ppermute x3, waiting for transfers between devices, shifted(): lax.ppermute(value, axis, [(source, source + steps) for source in range(i...  15 us
    ppermute x3, starting transfers between devices, shifted(): lax.ppermute(value, axis, [(source, source + steps) for source in range(i...  8.4 us
    dot_general x1, matrix products, on_device(): jnp.einsum('naij,njac->niac', window_probs, near_values, preferred_elemen...  6.4 us
  transfers between devices with their start and end apart: 5, of which 3 were waited for; matrix products, arithmetic and copies ran while one was open for 11% of the time, Pallas kernels for 0%

commit v1 on v0

--- a/solution.py
+++ b/solution.py
@@ -123,7 +123,8 @@
     zero_state = jnp.zeros(sent_state.shape, jnp.float32)
     group_sum = None
     inner_prefix = carried_in(sent_state, "inner", add_states, zero_state)
-    group_sum = lax.psum(sent_state, "inner")
+    blocks = lax.all_gather(sent_state, "inner")
+    group_sum = jnp.sum(blocks, axis=0)
     outer_before = carried_in(group_sum, "outer", add_states, zero_state)
     carried = inner_prefix + outer_before
     carried = carried.reshape(PHI, HEADS, VDIM)

time: 262 us -> 312 us (1.19)
  waiting for transfers between devices: 116 us -> 189 us
  blocking collectives: 29.1 us -> 0 us
    all_gather x0 -> x1, waiting for transfers between devices: none -> 62.5 us  [on_device(): blocks = lax.all_gather(sent_state, 'inner')]
    psum x1 -> x0, blocking collectives: 29.1 us -> none  [on_device(): group_sum = lax.psum(sent_state, 'inner')]
    all_gather x2, waiting for transfers between devices: 101 us -> 122 us  [carried_in(): everything = lax.all_gather(shard.astype(jnp.bfloat16), axis)]
    ppermute x3, waiting for transfers between devices: 15 us -> 4.33 us  [shifted(): lax.ppermute(value, axis, [(source, source + steps) for source in range(i...]
  transfers between devices with their start and end apart: 5 -> 6, of which waited for: 3 -> 4; matrix products, arithmetic and copies ran while one was open for 11% -> 11% of each run, Pallas kernels for 0% -> 0%
where the time goes in v1:
time: 312 us; the launch traced here: 310 us
  waiting for transfers between devices  189 us (61%)
  other arithmetic  69.5 us (22%)
  local copies, waits for them, and re-layouts  15.7 us (5%)
  between operations  13.5 us (4%)
  matrix products  11.8 us (4%)
  starting transfers between devices  9.55 us (3%)
    all_gather x2, waiting for transfers between devices, carried_in(): everything = lax.all_gather(shard.astype(jnp.bfloat16), axis)  122 us
    all_gather x1, waiting for transfers between devices, on_device(): blocks = lax.all_gather(sent_state, 'inner')  62.5 us
    select_n x36, other arithmetic, hop(): return jnp.where(reached, new, before)  60.4 us
    ppermute x3, starting transfers between devices, shifted(): lax.ppermute(value, axis, [(source, source + steps) for source in range(i...  9.47 us
    dot_general x1, matrix products, on_device(): jnp.einsum('naij,njac->niac', window_probs, near_values, preferred_elemen...  6.38 us
  transfers between devices with their start and end apart: 6, of which 4 were waited for; matrix products, arithmetic and copies ran while one was open for 11% of the time, Pallas kernels for 0%

profile of v1, /device:TPU:1, one launch (start us, length us, event | category | flops | bytes accessed | tf_op | source)
XLA Modules:
  0.0 309.8 jit_solution(4261989005177549827)
XLA Ops:
  7.5 3.9 %collective-permute-start = (bf16[2,1024]{0,1:T(8,128)(2,1)S(1)}, bf16[2,1024]{0,1:T(8,128)(2,1)S(1)}, u32[]{:S(2)}, u32[]{:S(2)}) collective-permute-start(bf16[2,1024]{0,1:T(8,128)(2,1)S(1)} %copy.66), channel_id=1, source_target_pairs={{0,1},{1,2},{2,3},{3,4},{4,5},{5,6},{6,7},{7,8},{8,9},{9,10},{10,1... | collective-permute-start | bytes 12296 | tf_op jit(solution)/shard_map/ppermute | solution.py:19
  13.0 4.3 %collective-permute-done = bf16[2,1024]{0,1:T(8,128)(2,1)S(1)} collective-permute-done((bf16[2,1024]{0,1:T(8,128)(2,1)S(1)}, bf16[2,1024]{0,1:T(8,128)(2,1)S(1)}, u32[]{:S(2)}, u32[]{:S(2)}) %collective-permute-start) | collective-permute-done | bytes 4128 | tf_op jit(solution)/shard_map/ppermute | solution.py:19
  22.5 62.5 %all-gather.8.cloned.1.call-done = f32[4,273,1024]{2,1,0:T(8,128)} async-done(((f32[1,273,1024]{2,1,0:T(8,128)}), f32[4,273,1024]{2,1,0:T(8,128)}) %all-gather.8.cloned.1.call-update) | async-done | bytes 4472848 | tf_op jit(solution)/shard_map/all_gather | solution.py:126
  85.0 2.8 reduce_sum.27
  90.1 2.5 collective-permute-start.1
  92.6 3.0 collective-permute-start.2
  102.3 2.6 fusion.77
  106.5 6.4 %convolution_bitcast_fusion = f32[2,64,16,64]{1,3,2,0:T(8,128)} fusion(bf16[2,64,16,64]{1,3,2,0:T(8,128)(2,1)} %copy.81, bf16[2,64,16,64]{1,3,2,0:T(8,128)(2,1)S(1)} %copy.80, f32[2,16,64]{2,1,0:T(8,128)} %fusion.77, pred[2,64,128]{2,1,0:T(8,128)(4,1)S(1)} %broadcast_and_fusion, bf16[2,64,16,16]{1,3,2,0:T(8,128)(2,1)} %copy.85, ...), kind=kOutput, calls=%fused_computation.8 | convolution fusion | flops 44828800 | bytes 1269760 | tf_op jit(solution)/shard_map/naij,njac->niac/dot_general | solution.py:119
  112.8 2.1 copy.95
  116.3 11.5 %all-gather.6.cloned.1.call-done = bf16[4,273,1024]{2,1,0:T(8,128)(2,1)} async-done(((bf16[1,273,1024]{2,1,0:T(8,128)(2,1)}), bf16[4,273,1024]{2,1,0:T(8,128)(2,1)}) %all-gather.6.cloned.1.call-update) | async-done | bytes 2236432 | tf_op jit(solution)/shard_map/all_gather | solution.py:24
  127.8 6.8 %while.28 = (s32[]{:T(128)}, f32[273,1024]{1,0:T(8,128)S(1)}, s32[]{:T(128)}, bf16[4,273,1024]{2,1,0:T(8,128)(2,1)}, s32[]{:T(128)}, /*index=5*/s32[]{:T(128)}) while((s32[]{:T(128)}, f32[273,1024]{1,0:T(8,128)S(1)}, s32[]{:T(128)}, bf16[4,273,1024]{2,1,0:T(8,128)(2,1)}, s32[]{:T(128)}, /*index=5*/s32[]{:T(128)}) %tuple.62), condition=%wide.region_1.2_spmd.clone, body=%wide.region_0.1_spmd.clone.sunk | while | flops 1118212 | bytes 2795613 | solution.py:32
  127.8 1.7 add_select_fusion.4
  129.5 1.7 add_select_fusion.4
  131.2 1.7 add_select_fusion.4
  132.9 1.7 add_select_fusion.4
  134.6 110.6 %all-gather.10.cloned.1.call-done = bf16[32,273,1024]{2,1,0:T(8,128)(2,1)} async-done(((bf16[1,273,1024]{2,1,0:T(8,128)(2,1)}), bf16[32,273,1024]{2,1,0:T(8,128)(2,1)}) %all-gather.10.cloned.1.call-update) | async-done | bytes 17891344 | tf_op jit(solution)/shard_map/all_gather | solution.py:24
  245.2 54.4 %while.29 = (s32[]{:T(128)}, f32[273,1024]{1,0:T(8,128)S(1)}, s32[]{:T(128)}, bf16[32,273,1024]{2,1,0:T(8,128)(2,1)}, s32[]{:T(128)}, /*index=5*/s32[]{:T(128)}) while((s32[]{:T(128)}, f32[273,1024]{1,0:T(8,128)S(1)}, s32[]{:T(128)}, bf16[32,273,1024]{2,1,0:T(8,128)(2,1)}, s32[]{:T(128)}, /*index=5*/s32[]{:T(128)}) %tuple.65), condition=%wide.region_4.5_spmd.clone, body=%wide.region_3.4_spmd.clone.sunk | while | flops 1118212 | bytes 2795613 | solution.py:32
  246.9 1.7 add_select_fusion.5
  248.6 1.7 add_select_fusion.5
  250.3 1.7 add_select_fusion.5
  252.0 1.7 add_select_fusion.5
  253.7 1.7 add_select_fusion.5
  255.4 1.7 add_select_fusion.5
  257.1 1.7 add_select_fusion.5
  258.8 1.7 add_select_fusion.5
  260.5 1.7 add_select_fusion.5
  262.2 1.7 add_select_fusion.5
  263.9 1.7 add_select_fusion.5
  265.6 1.7 add_select_fusion.5
  267.3 1.7 add_select_fusion.5
  269.0 1.7 add_select_fusion.5
  270.7 1.7 add_select_fusion.5
  272.4 1.7 add_select_fusion.5
  274.1 1.7 add_select_fusion.5
  275.8 1.7 add_select_fusion.5
  277.5 1.7 add_select_fusion.5
  279.2 1.7 add_select_fusion.5
  280.9 1.7 add_select_fusion.5
  282.6 1.7 add_select_fusion.5
  284.3 1.7 add_select_fusion.5
  286.0 1.7 add_select_fusion.5
  287.7 1.7 add_select_fusion.5
  289.4 1.7 add_select_fusion.5
  291.1 1.7 add_select_fusion.5
  292.8 1.7 add_select_fusion.5
  294.5 1.7 add_select_fusion.5
  296.2 1.7 add_select_fusion.5
  297.9 1.7 add_select_fusion.5
  (85 shorter events, 24.4 us)
Async XLA Ops:
  6.5 6.3 %copy-start.4 = (bf16[128,1024]{1,0:T(8,128)(2,1)S(1)}, bf16[128,1024]{1,0:T(8,128)(2,1)}, u32[]{:S(2)}) copy-start(bf16[128,1024]{1,0:T(8,128)(2,1)} %param.11) | copy-start | bytes 786436
  6.5 6.3 %copy-start.9 = (f32[3,1024]{1,0:T(4,128)S(1)}, f32[3,1024]{1,0:T(4,128)}, u32[]{:S(2)}) copy-start(f32[3,1024]{1,0:T(4,128)} %param.12) | copy-start | bytes 36868
  6.5 78.5 %all-gather.8.cloned.1.call-start = ((), (), s32[]{:S(2)}) async-start(), calls=%async_computation.1 | async-start | bytes 5734400 | tf_op jit(solution)/shard_map/all_gather | solution.py:126
  7.5 9.8 %collective-permute-start = (bf16[2,1024]{0,1:T(8,128)(2,1)S(1)}, bf16[2,1024]{0,1:T(8,128)(2,1)S(1)}, u32[]{:S(2)}, u32[]{:S(2)}) collective-permute-start(bf16[2,1024]{0,1:T(8,128)(2,1)S(1)} %copy.66), channel_id=1, source_target_pairs={{0,1},{1,2},{2,3},{3,4},{4,5},{5,6},{6,7},{7,8},{8,9},{9,10},{10,1... | collective-permute-start | bytes 12296 | tf_op jit(solution)/shard_map/ppermute | solution.py:19
  13.0 5.7 %copy-start.11 = (bf16[273]{0:T(512)(128)(2,1)}, bf16[273]{0:T(512)(128)(2,1)S(1)}, u32[]{:S(2)}) copy-start(bf16[273]{0:T(512)(128)(2,1)S(1)} %pad.11.clone) | copy-start | bytes 1642
  20.2 1.3 copy-start
  20.3 107.5 %all-gather.6.cloned.1.call-start = ((), (), s32[]{:S(2)}) async-start(), calls=%async_computation | async-start | bytes 2867200 | tf_op jit(solution)/shard_map/all_gather | solution.py:24
  22.4 222.7 %all-gather.10.cloned.1.call-start = ((), (), s32[]{:S(2)}) async-start(), calls=%async_computation.2 | async-start | bytes 18923520 | tf_op jit(solution)/shard_map/all_gather | solution.py:24
  89.4 3.3 %copy-start.3 = (bf16[128,256]{1,0:T(8,128)(2,1)S(1)}, bf16[128,256]{1,0:T(8,128)(2,1)}, u32[]{:S(2)}) copy-start(bf16[128,256]{1,0:T(8,128)(2,1)} %param.10) | copy-start | bytes 196612
  89.4 6.4 %copy-start.7 = (bf16[128,256]{1,0:T(8,128)(2,1)S(1)}, bf16[128,256]{1,0:T(8,128)(2,1)}, u32[]{:S(2)}) copy-start(bf16[128,256]{1,0:T(8,128)(2,1)} %param.9) | copy-start | bytes 196612
  90.1 14.9 %collective-permute-start.1 = (bf16[64,1024]{0,1:T(8,128)(2,1)S(1)}, bf16[64,1024]{0,1:T(8,128)(2,1)}, u32[]{:S(2)}, u32[]{:S(2)}) collective-permute-start(bf16[64,1024]{0,1:T(8,128)(2,1)S(1)} %add_convert_fusion.1), channel_id=1, source_target_pairs={{0,1},{1,2},{2,3},{3,4},{4,5},{5,6},{6,7},{7,8},{8,9},{9,10},{10,1... | collective-permute-start | bytes 393224 | tf_op jit(solution)/shard_map/ppermute | solution.py:19
  92.6 9.4 %collective-permute-start.2 = (bf16[64,256]{1,0:T(8,128)(2,1)S(1)}, bf16[64,256]{1,0:T(8,128)(2,1)S(1)}, u32[]{:S(2)}, u32[]{:S(2)}) collective-permute-start(bf16[64,256]{1,0:T(8,128)(2,1)S(1)} %slice.69), channel_id=1, source_target_pairs={{0,1},{1,2},{2,3},{3,4},{4,5},{5,6},{6,7},{7,8},{8,9},{9,10},{10,1... | collective-permute-start | bytes 98312 | tf_op jit(solution)/shard_map/ppermute | solution.py:19
  102.3 2.6 copy-start.6
  104.9 1.5 copy-start.5
  299.6 1.0 copy-start.13
  299.8 1.3 copy-start.2
  299.9 1.3 copy-start.8
  299.9 1.2 copy-start.12
  301.1 1.0 copy-start.1
  301.1 1.0 copy-start.10
Sparse Core Ops, SparseCore 0:
  20.4 64.5 all-gather.7
  87.1 40.5 all-gather.5
  129.9 115.2 all-gather.9
